TPU v7x, 512 devices: a whole 4x4x16 slice. The times are simulated.
512 devices in a mesh: dp: 2 (over core), row: 16 (over y, z_lo), col: 16 (over z_hi, x).
Axes of the slice: x: 4, y: 4, z: 16 (z_hi: 4, z_lo: 4; z = z_hi * 4 + z_lo), core: 2. Of those that a mesh axis runs over, the one named last changes fastest.
Arguments:
- queries: bfloat16 [2, 2048, 4096], P('dp', 'row', 'col'), may hold values from -6 to 6
- key_vectors: bfloat16 [2, 2048, 4096], P('dp', 'row', 'col'), may hold values from -6 to 6
- value_vectors: bfloat16 [2, 2048, 4096], P('dp', 'row', 'col'), may hold values from -6 to 6
- out_weight: bfloat16 [4096, 3072], P('row', 'col'), may hold values from -0.09375 to 0.09375
- out_grad: bfloat16 [2, 2048, 3072], P('dp', 'row', 'col'), may hold values from -6 to 6
Outputs:
- output: bfloat16 [2, 2048, 3072], P('dp', 'row', 'col')
- grad_queries: bfloat16 [2, 2048, 4096], P('dp', 'row', 'col')
- grad_keys: bfloat16 [2, 2048, 4096], P('dp', 'row', 'col')
- grad_values: bfloat16 [2, 2048, 4096], P('dp', 'row', 'col')
- grad_weight: float32 [4096, 3072], P(('dp', 'row'), 'col')
All inputs are finite; a program needn't handle non-finite values.
Results may differ from a plain program's by a relative error of at most 0.038.
Values may be sent and summed in bfloat16 or wider, within the bound.
A program may use at most 64 MiB of HBM per device.

v0:
```python
import math
import jax
import jax.numpy as jnp
from jax import lax
from jax.sharding import PartitionSpec as P

HEAD = 128
NEG = -1e30


def split_heads(array_in):
    return array_in.reshape(array_in.shape[0], array_in.shape[1] // HEAD, HEAD)


def merge_heads(array_in):
    return array_in.reshape(array_in.shape[0], array_in.shape[1] * array_in.shape[2])


def causal_scores(query_part, key_part, query_first, key_first):
    scores = jnp.einsum(
        "qhe,khe->qhk", query_part, key_part, preferred_element_type=jnp.float32
    ) * (1.0 / math.sqrt(HEAD))
    query_pos = query_first + lax.broadcasted_iota(jnp.int32, (query_part.shape[0], 1, 1), 0)
    key_pos = key_first + lax.broadcasted_iota(jnp.int32, (1, 1, key_part.shape[0]), 2)
    visible = key_pos <= query_pos
    return (jnp.where(visible, scores, NEG), visible)


def shards(queries, key_vectors, value_vectors, out_weight, out_grad):
    own_rows = queries.shape[1]
    heads_local = queries.shape[2] // HEAD
    own_first = lax.axis_index("row") * own_rows
    own_queries = split_heads(queries[0])
    own_keys = split_heads(key_vectors[0])
    own_values = split_heads(value_vectors[0])
    grad_local = out_grad[0]
    portion = (
        lax.all_gather(key_vectors[0], "row", axis=0, tiled=True),
        lax.all_gather(value_vectors[0], "row", axis=0, tiled=True),
    )
    running_max = jnp.full((own_rows, heads_local), NEG, jnp.float32)
    key_part = split_heads(portion[0])
    value_part = split_heads(portion[1]).astype(jnp.float32)
    scores, visible = causal_scores(own_queries, key_part, own_first, jnp.int32(0))
    new_max = jnp.maximum(running_max, jnp.max(scores, axis=2))
    weights = jnp.where(visible, jnp.exp(scores - new_max[:, :, None]), 0.0)
    running_sum = jnp.sum(weights, axis=2)
    accumulated = jnp.einsum(
        "qhk,khe->qhe",
        weights,
        value_part,
        precision=lax.Precision.HIGHEST,
        preferred_element_type=jnp.float32,
    )
    running_max, running_sum, accumulated = (new_max, running_sum, accumulated)
    attended = merge_heads(accumulated / running_sum[:, :, None]).astype(jnp.bfloat16)
    log_norm = running_max + jnp.log(running_sum)
    attn_full = lax.all_gather(attended, "col", axis=1, tiled=True)
    columns = attn_full
    output_rows = jnp.dot(
        columns,
        lax.all_gather(out_weight, "row", axis=0, tiled=True),
        preferred_element_type=jnp.float32,
    )
    head_terms = lax.dot_general(
        grad_local,
        lax.all_gather(out_weight, "row", axis=0, tiled=True),
        (((1,), (1,)), ((), ())),
        preferred_element_type=jnp.float32,
    )
    grad_attended = lax.psum_scatter(
        head_terms.astype(jnp.bfloat16), "col", scatter_dimension=1, tiled=True
    )
    upstream_own = split_heads(grad_attended)
    row_dot = jnp.sum(
        upstream_own.astype(jnp.float32) * split_heads(attended).astype(jnp.float32), axis=2
    )
    portion = (
        lax.all_gather(key_vectors[0], "row", axis=0, tiled=True),
        lax.all_gather(value_vectors[0], "row", axis=0, tiled=True),
    )
    key_part = split_heads(portion[0])
    value_part = split_heads(portion[1])
    scores, visible = causal_scores(own_queries, key_part, own_first, jnp.int32(0))
    attention = jnp.where(visible, jnp.exp(scores - log_norm[:, :, None]), 0.0)
    grad_probs = jnp.einsum(
        "qhe,khe->qhk", upstream_own, value_part, preferred_element_type=jnp.float32
    )
    grad_scores = (attention * (grad_probs - row_dot[:, :, None])).astype(jnp.bfloat16)
    grad_query_sum = jnp.einsum(
        "qhk,khe->qhe", grad_scores, key_part, preferred_element_type=jnp.float32
    )
    grad_queries = merge_heads(grad_query_sum * (1.0 / math.sqrt(HEAD))).astype(jnp.bfloat16)
    sent = (queries[0].astype(jnp.float32), grad_attended.astype(jnp.float32), log_norm, row_dot)
    portion = (
        lax.all_gather(sent[0], "row", axis=0, tiled=True),
        lax.all_gather(sent[1], "row", axis=0, tiled=True),
        lax.all_gather(sent[2], "row", axis=0, tiled=True),
        lax.all_gather(sent[3], "row", axis=0, tiled=True),
    )
    query_part = split_heads(portion[0].astype(jnp.bfloat16))
    upstream = split_heads(portion[1].astype(jnp.bfloat16))
    norm_part = portion[2]
    dot_part = portion[3]
    scores, visible = causal_scores(query_part, own_keys, jnp.int32(0), own_first)
    attention = jnp.where(visible, jnp.exp(scores - norm_part[:, :, None]), 0.0)
    grad_value_sum = jnp.einsum(
        "qhk,qhe->khe", attention.astype(jnp.bfloat16), upstream, preferred_element_type=jnp.float32
    )
    grad_probs = jnp.einsum(
        "qhe,khe->qhk", upstream, own_values, preferred_element_type=jnp.float32
    )
    grad_scores = (attention * (grad_probs - dot_part[:, :, None])).astype(jnp.bfloat16)
    grad_key_sum = jnp.einsum(
        "qhk,qhe->khe", grad_scores, query_part, preferred_element_type=jnp.float32
    )
    grad_key_sum, grad_value_sum = (grad_key_sum, grad_value_sum)
    grad_keys = merge_heads(grad_key_sum * (1.0 / math.sqrt(HEAD))).astype(jnp.bfloat16)
    grad_values = merge_heads(grad_value_sum).astype(jnp.bfloat16)
    columns = attn_full
    grad_weight = lax.psum_scatter(
        lax.dot_general(
            columns, grad_local, (((0,), (0,)), ((), ())), preferred_element_type=jnp.float32
        ),
        ("dp", "row"),
        scatter_dimension=0,
        tiled=True,
    )
    return (
        output_rows.astype(jnp.bfloat16)[None],
        grad_queries[None],
        grad_keys[None],
        grad_values[None],
        grad_weight,
    )


def solution(mesh):
    return jax.shard_map(
        shards,
        mesh=mesh,
        in_specs=(
            P("dp", "row", "col"),
            P("dp", "row", "col"),
            P("dp", "row", "col"),
            P("row", "col"),
            P("dp", "row", "col"),
        ),
        out_specs=(
            P("dp", "row", "col"),
            P("dp", "row", "col"),
            P("dp", "row", "col"),
            P("dp", "row", "col"),
            P(("dp", "row"), "col"),
        ),
        check_vma=False,
    )
```

profile of v0, /device:TPU:1, one launch (start us, length us, event | category | flops | bytes accessed | tf_op | source)
XLA Modules:
  0.0 794.0 jit_solution(7137687552195433287)
XLA Ops:
  7.2 0.0 copy-start
  7.2 0.0 copy-start.4
  7.2 0.0 all-gather.12.cloned.1.call-start
  7.2 0.7 all-gather.12.cloned.1.call-update
  7.9 0.0 all-gather.18.cloned.1.call-start
  8.0 0.7 all-gather.18.cloned.1.call-update
  8.7 0.0 all-gather.16.cloned.1.call-start
  8.7 1.6 copy.24
  10.3 0.0 all-gather.16.cloned.1.call-update
  10.3 0.0 reduce-scatter.3.cloned.1.call-start
  10.4 78.9 %all-gather.12.cloned.1.call-done = bf16[4096,192]{0,1:T(8,128)(2,1)} async-done(((bf16[256,192]{0,1:T(8,128)(2,1)}), bf16[4096,192]{0,1:T(8,128)(2,1)}) %all-gather.12.cloned.1.call-update) | async-done | bytes 1572880 | tf_op jit(solution)/shard_map/all_gather | solution.py:62
  89.2 0.0 copy-done
  89.2 2.8 convolution_convert_fusion
  92.1 0.0 reduce-scatter.3.cloned.1.call-update
  92.1 0.0 all-gather.10.cloned.1.call-start
  92.1 0.0 copy-done.4
  92.2 0.2 iota_compare_fusion.1
  92.4 85.0 %all-gather.18.cloned.1.call-done = bf16[1,2048,256]{2,1,0:T(8,128)(2,1)} async-done(((bf16[1,128,256]{2,1,0:T(8,128)(2,1)}), bf16[1,2048,256]{2,1,0:T(8,128)(2,1)}) %all-gather.18.cloned.1.call-update) | async-done | bytes 1048592 | tf_op jit(solution)/shard_map/all_gather | solution.py:39
  177.4 1.5 copy.27
  178.9 0.0 copy-start.3
  178.9 76.4 %all-gather.16.cloned.1.call-done = bf16[1,2048,256]{1,2,0:T(8,128)(2,1)} async-done(((bf16[1,128,256]{1,2,0:T(8,128)(2,1)}), bf16[1,2048,256]{1,2,0:T(8,128)(2,1)}) %all-gather.16.cloned.1.call-update) | async-done | bytes 1048592 | tf_op jit(solution)/shard_map/all_gather | solution.py:38
  255.2 1.9 fusion.41
  257.1 0.4 fusion.13
  257.6 122.3 %reduce-scatter.3.cloned.1.call-done = bf16[128,256]{1,0:T(8,128)(2,1)} async-done(((bf16[128,4096]{1,0:T(8,128)(2,1)}), bf16[128,256]{1,0:T(8,128)(2,1)}) %reduce-scatter.3.cloned.1.call-update) | async-done | bytes 65552 | tf_op jit(solution)/shard_map/reduce_scatter | solution.py:71
  379.9 1.6 copy.29
  381.4 0.0 copy-done.3
  381.4 0.0 copy-start.5
  381.4 3.1 multiply_reduce_fusion
  384.6 0.0 all-gather.10.cloned.1.call-update
  384.6 0.0 all-gather.20.cloned.1.call-start
  384.6 0.0 copy-done.5
  384.6 0.7 copy.31
  385.4 0.0 all-gather.20.cloned.1.call-update
  385.4 0.0 all-gather.14.cloned.1.call-start
  385.5 0.7 all-gather.14.cloned.1.call-update
  386.2 0.0 reduce-scatter.5.cloned.1.call-start
  386.2 71.2 %all-gather.10.cloned.1.call-done = bf16[128,4096]{0,1:T(8,128)(2,1)} async-done(((bf16[128,256]{0,1:T(8,128)(2,1)}), bf16[128,4096]{0,1:T(8,128)(2,1)}) %all-gather.10.cloned.1.call-update) | async-done | bytes 1048592 | tf_op jit(solution)/shard_map/all_gather | solution.py:58
  457.4 3.4 fusion.36
  460.8 0.0 copy-start.6
  460.8 0.0 copy-start.7
  460.8 0.0 reduce-scatter.5.cloned.1.call-update
  460.9 0.8 copy-done.6
  461.7 0.6 reshape_squeeze.10
  462.3 0.0 copy-done.7
  462.3 0.1 copy.48
  462.4 0.9 iota_compare_fusion
  463.4 33.1 %all_gather.32 = f32[2048,2]{0,1:T(2,128)S(1)} all-gather(f32[128,2]{0,1:T(2,128)S(1)} %log_add_fusion), channel_id=1, replica_groups=mesh['dp'=2,'row'=16,'col'=16] {'row'}, dimensions={0}, use_global_device_ids=true | all-gather | bytes 17408 | tf_op jit(solution)/shard_map/all_gather | solution.py:98
  496.4 25.6 %all-gather.20.cloned.1.call-done = bf16[1,2048,256]{1,2,0:T(8,128)(2,1)} async-done(((bf16[1,128,256]{1,2,0:T(8,128)(2,1)}), bf16[1,2048,256]{1,2,0:T(8,128)(2,1)}) %all-gather.20.cloned.1.call-update) | async-done | bytes 1048592 | tf_op jit(solution)/shard_map/all_gather | solution.py:96
  522.1 0.0 copy-start.2
  522.1 3.6 fusion.8
  525.6 0.0 copy-done.2
  525.6 3.0 fusion.21
  528.7 0.0 copy-start.1
  528.7 1.7 copy.37
  530.4 35.5 %all_gather.34 = f32[2048,2]{0,1:T(2,128)S(1)} all-gather(f32[128,2]{0,1:T(2,128)S(1)} %get-tuple-element.17), channel_id=1, replica_groups=mesh['dp'=2,'row'=16,'col'=16] {'row'}, dimensions={0}, use_global_device_ids=true | all-gather | bytes 17408 | tf_op jit(solution)/shard_map/all_gather | solution.py:99
  565.9 44.3 %all-gather.14.cloned.1.call-done = bf16[2048,256]{1,0:T(8,128)(2,1)} async-done(((bf16[128,256]{1,0:T(8,128)(2,1)}), bf16[2048,256]{1,0:T(8,128)(2,1)}) %all-gather.14.cloned.1.call-update) | async-done | bytes 1048592 | tf_op jit(solution)/shard_map/all_gather | solution.py:97
  610.2 1.5 copy.49
  611.7 0.0 copy-done.1
  611.7 2.0 fusion.23
  613.7 0.7 copy.38
  614.4 0.4 convolution_convert_fusion.1
  614.9 0.7 copy.39
  615.6 2.9 fusion.24
  618.5 168.6 %reduce-scatter.5.cloned.1.call-done = f32[128,192]{0,1:T(8,128)} async-done(((f32[4096,192]{0,1:T(8,128)}), f32[128,192]{0,1:T(8,128)}) %reduce-scatter.5.cloned.1.call-update) | async-done | bytes 98320 | tf_op jit(solution)/shard_map/reduce_scatter | solution.py:121
  (4 shorter events, 0.0 us)
Async XLA Ops:
  7.2 82.1 %copy-start = (bf16[1,128,192]{1,2,0:T(8,128)(2,1)S(1)}, bf16[1,128,192]{1,2,0:T(8,128)(2,1)}, u32[]{:S(2)}) copy-start(bf16[1,128,192]{1,2,0:T(8,128)(2,1)} %param.9) | copy-start | bytes 147460
  7.2 85.0 %copy-start.4 = (bf16[1,128,256]{2,1,0:T(8,128)(2,1)S(1)}, bf16[1,128,256]{2,1,0:T(8,128)(2,1)}, u32[]{:S(2)}) copy-start(bf16[1,128,256]{2,1,0:T(8,128)(2,1)} %param.5) | copy-start | bytes 196612
  7.2 82.0 %all-gather.12.cloned.1.call-start = ((), (), s32[]{:S(2)}) async-start(), calls=%async_computation.3 | async-start | bytes 1671168 | tf_op jit(solution)/shard_map/all_gather | solution.py:62
  7.9 169.4 %all-gather.18.cloned.1.call-start = ((), (), s32[]{:S(2)}) async-start(), calls=%async_computation.8 | async-start | bytes 1114112 | tf_op jit(solution)/shard_map/all_gather | solution.py:39
  8.7 246.6 %all-gather.16.cloned.1.call-start = ((), (), s32[]{:S(2)}) async-start(), calls=%async_computation.7 | async-start | bytes 1114112 | tf_op jit(solution)/shard_map/all_gather | solution.py:38
  10.3 369.5 %reduce-scatter.3.cloned.1.call-start = ((), (), s32[]{:S(2)}) async-start(), calls=%async_computation.4 | async-start | bytes 1114112 | tf_op jit(solution)/shard_map/reduce_scatter | solution.py:71
  92.1 365.3 %all-gather.10.cloned.1.call-start = ((), (), s32[]{:S(2)}) async-start(), calls=%async_computation.2 | async-start | bytes 1114112 | tf_op jit(solution)/shard_map/all_gather | solution.py:58
  178.9 202.6 %copy-start.3 = (bf16[1,2048,256]{1,2,0:T(8,128)(2,1)}, bf16[1,2048,256]{1,2,0:T(8,128)(2,1)S(1)}, u32[]{:S(2)}) copy-start(bf16[1,2048,256]{1,2,0:T(8,128)(2,1)S(1)} %copy.27) | copy-start | bytes 3145732
  381.4 3.2 copy-start.5
  384.6 137.5 %all-gather.20.cloned.1.call-start = ((), (), s32[]{:S(2)}) async-start(), calls=%async_computation.9 | async-start | bytes 1114112 | tf_op jit(solution)/shard_map/all_gather | solution.py:96
  385.4 224.8 %all-gather.14.cloned.1.call-start = ((), (), s32[]{:S(2)}) async-start(), calls=%async_computation.5 | async-start | bytes 1114112 | tf_op jit(solution)/shard_map/all_gather | solution.py:97
  386.2 401.0 %reduce-scatter.5.cloned.1.call-start = ((), (), s32[]{:S(2)}) async-start(), calls=%async_computation.6 | async-start | bytes 3244032 | tf_op jit(solution)/shard_map/reduce_scatter | solution.py:121
  460.8 0.8 copy-start.6
  460.8 1.5 copy-start.7
  522.1 3.6 copy-start.2
  528.7 83.0 %copy-start.1 = (f32[2048,2,128]{0,2,1:T(8,128)S(1)}, f32[2048,2,128]{0,2,1:T(8,128)}, u32[]{:S(2)}) copy-start(f32[2048,2,128]{0,2,1:T(8,128)} %fusion.8) | copy-start | bytes 6291460
Sparse Core Ops, SparseCore 0:
  10.0 79.1 all-gather.11
  91.3 86.0 all-gather.17
  179.9 75.2 all-gather.15
  259.2 120.6 reduce-scatter.2
  384.7 72.6 all-gather.9
  460.0 61.9 all-gather.19
  524.4 85.7 all-gather.13
  613.8 173.2 reduce-scatter.4
where the time goes:
time: 795 us; the launch traced here: 794 us
  waiting for transfers between devices  674 us (85%)
  blocking collectives  68.5 us (9%)
  matrix products  23.2 us (3%)
  between operations  14.3 us (2%)
  local copies, waits for them, and re-layouts  11.7 us (1%)
    reduce_scatter x1, waiting for transfers between devices, shards(): lax.psum_scatter(lax.dot_general(columns, grad_local, (((0,), (0,)), ((),...  169 us
    reduce_scatter x1, waiting for transfers between devices, shards(): lax.psum_scatter(head_terms.astype(jnp.bfloat16), 'col', scatter_dimensio...  122 us
    all_gather x1, waiting for transfers between devices, shards(): lax.all_gather(value_vectors[0], 'row', axis=0, tiled=True)  85 us
    all_gather x1, waiting for transfers between devices, shards(): lax.all_gather(out_weight, 'row', axis=0, tiled=True)  78.9 us
    all_gather x1, waiting for transfers between devices, shards(): lax.all_gather(key_vectors[0], 'row', axis=0, tiled=True)  76.4 us
    all_gather x1, waiting for transfers between devices, shards(): attn_full = lax.all_gather(attended, 'col', axis=1, tiled=True)  71.2 us
    all_gather x1, waiting for transfers between devices, shards(): lax.all_gather(sent[1], 'row', axis=0, tiled=True)  44.3 us
    all_gather x1, blocking collectives, shards(): lax.all_gather(sent[3], 'row', axis=0, tiled=True)  35.5 us
  transfers between devices with their start and end apart: 8, of which 8 were waited for; matrix products, arithmetic and copies ran while one was open for 4% of the time, Pallas kernels for 0%

commit v1 on v0

--- a/solution.py
+++ b/solution.py
@@ -96,7 +96,9 @@
         lax.all_gather(sent[0], "row", axis=0, tiled=True),
         lax.all_gather(sent[1], "row", axis=0, tiled=True),
         lax.all_gather(sent[2], "row", axis=0, tiled=True),
-        lax.all_gather(sent[3], "row", axis=0, tiled=True),
+        jnp.concatenate(
+            lax.all_to_all(jnp.stack([sent[3]] * lax.axis_size("row")), "row", 0, 0), axis=0
+        ),
     )
     query_part = split_heads(portion[0].astype(jnp.bfloat16))
     upstream = split_heads(portion[1].astype(jnp.bfloat16))

time: 795 us -> 794 us (level)
  blocking collectives: 68.5 us -> 33.3 us
  waiting for transfers between devices: 674 us -> 702 us
    all_gather x1 -> x0, blocking collectives: 35.5 us -> none  [shards(): lax.all_gather(sent[3], 'row', axis=0, tiled=True)]
    all_gather x1, waiting for transfers between devices: 44.3 us -> 71.8 us  [shards(): lax.all_gather(sent[1], 'row', axis=0, tiled=True)]
  transfers between devices with their start and end apart: 8 -> 9, of which waited for: 8 -> 8; matrix products, arithmetic and copies ran while one was open for 4% -> 4% of each run, Pallas kernels for 0% -> 0%
where the time goes in v1:
time: 794 us; the launch traced here: 793 us
  waiting for transfers between devices  702 us (88%)
  blocking collectives  33.3 us (4%)
  matrix products  23.1 us (3%)
  between operations  14.3 us (2%)
  local copies, waits for them, and re-layouts  12.2 us (2%)
    reduce_scatter x1, waiting for transfers between devices, shards(): lax.psum_scatter(lax.dot_general(columns, grad_local, (((0,), (0,)), ((),...  168 us
    reduce_scatter x1, waiting for transfers between devices, shards(): lax.psum_scatter(head_terms.astype(jnp.bfloat16), 'col', scatter_dimensio...  122 us
    all_gather x1, waiting for transfers between devices, shards(): lax.all_gather(value_vectors[0], 'row', axis=0, tiled=True)  85 us
    all_gather x1, waiting for transfers between devices, shards(): lax.all_gather(out_weight, 'row', axis=0, tiled=True)  78.9 us
    all_gather x1, waiting for transfers between devices, shards(): lax.all_gather(key_vectors[0], 'row', axis=0, tiled=True)  76.4 us
    all_gather x1, waiting for transfers between devices, shards(): lax.all_gather(sent[1], 'row', axis=0, tiled=True)  71.8 us
    all_gather x1, waiting for transfers between devices, shards(): attn_full = lax.all_gather(attended, 'col', axis=1, tiled=True)  71.2 us
    all_gather x1, blocking collectives, shards(): lax.all_gather(sent[2], 'row', axis=0, tiled=True)  33.3 us
  transfers between devices with their start and end apart: 9, of which 8 were waited for; matrix products, arithmetic and copies ran while one was open for 4% of the time, Pallas kernels for 0%

profile of v1, /device:TPU:1, one launch (start us, length us, event | category | flops | bytes accessed | tf_op | source)
XLA Modules:
  0.0 793.3 jit_solution(5351877498228340934)
XLA Ops:
  7.2 0.0 copy-start
  7.2 0.0 copy-start.4
  7.2 0.0 all-gather.12.cloned.1.call-start
  7.2 0.7 all-gather.12.cloned.1.call-update
  7.9 0.0 all-gather.18.cloned.1.call-start
  8.0 0.7 all-gather.18.cloned.1.call-update
  8.7 0.0 all-gather.16.cloned.1.call-start
  8.7 1.6 copy.40
  10.3 0.0 all-gather.16.cloned.1.call-update
  10.3 0.0 reduce-scatter.3.cloned.1.call-start
  10.4 78.9 %all-gather.12.cloned.1.call-done = bf16[4096,192]{0,1:T(8,128)(2,1)} async-done(((bf16[256,192]{0,1:T(8,128)(2,1)}), bf16[4096,192]{0,1:T(8,128)(2,1)}) %all-gather.12.cloned.1.call-update) | async-done | bytes 1572880 | tf_op jit(solution)/shard_map/all_gather | solution.py:62
  89.2 0.0 copy-done
  89.2 2.8 convolution_convert_fusion
  92.1 0.0 reduce-scatter.3.cloned.1.call-update
  92.1 0.0 all-gather.10.cloned.1.call-start
  92.1 0.0 copy-done.4
  92.2 0.2 iota_compare_fusion.1
  92.4 85.0 %all-gather.18.cloned.1.call-done = bf16[1,2048,256]{2,1,0:T(8,128)(2,1)} async-done(((bf16[1,128,256]{2,1,0:T(8,128)(2,1)}), bf16[1,2048,256]{2,1,0:T(8,128)(2,1)}) %all-gather.18.cloned.1.call-update) | async-done | bytes 1048592 | tf_op jit(solution)/shard_map/all_gather | solution.py:39
  177.4 1.5 copy.43
  178.9 0.0 copy-start.3
  178.9 76.4 %all-gather.16.cloned.1.call-done = bf16[1,2048,256]{1,2,0:T(8,128)(2,1)} async-done(((bf16[1,128,256]{1,2,0:T(8,128)(2,1)}), bf16[1,2048,256]{1,2,0:T(8,128)(2,1)}) %all-gather.16.cloned.1.call-update) | async-done | bytes 1048592 | tf_op jit(solution)/shard_map/all_gather | solution.py:38
  255.2 1.9 fusion.43
  257.1 0.4 fusion.13
  257.6 122.3 %reduce-scatter.3.cloned.1.call-done = bf16[128,256]{1,0:T(8,128)(2,1)} async-done(((bf16[128,4096]{1,0:T(8,128)(2,1)}), bf16[128,256]{1,0:T(8,128)(2,1)}) %reduce-scatter.3.cloned.1.call-update) | async-done | bytes 65552 | tf_op jit(solution)/shard_map/reduce_scatter | solution.py:71
  379.9 1.6 copy.45
  381.4 0.0 copy-done.3
  381.4 0.0 copy-start.5
  381.4 3.1 multiply_reduce_fusion
  384.6 0.0 all-gather.10.cloned.1.call-update
  384.6 0.0 all-gather.20.cloned.1.call-start
  384.6 0.0 copy-done.5
  384.6 0.7 copy.50
  385.4 0.0 all-gather.20.cloned.1.call-update
  385.4 0.0 all-gather.14.cloned.1.call-start
  385.5 0.7 all-gather.14.cloned.1.call-update
  386.2 0.0 reduce-scatter.5.cloned.1.call-start
  386.2 71.2 %all-gather.10.cloned.1.call-done = bf16[128,4096]{0,1:T(8,128)(2,1)} async-done(((bf16[128,256]{0,1:T(8,128)(2,1)}), bf16[128,4096]{0,1:T(8,128)(2,1)}) %all-gather.10.cloned.1.call-update) | async-done | bytes 1048592 | tf_op jit(solution)/shard_map/all_gather | solution.py:58
  457.4 3.4 fusion.38
  460.8 0.0 copy-start.6
  460.8 0.0 copy-start.7
  460.9 0.0 reduce-scatter.5.cloned.1.call-update
  460.9 0.8 copy-done.6
  461.7 0.6 reshape_squeeze.10
  462.3 0.0 copy-done.7
  462.4 0.9 iota_compare_fusion
  463.3 33.3 %all_gather.29 = f32[2048,2]{0,1:T(2,128)S(1)} all-gather(f32[128,2]{0,1:T(2,128)S(1)} %log_add_fusion), channel_id=1, replica_groups=mesh['dp'=2,'row'=16,'col'=16] {'row'}, dimensions={0}, use_global_device_ids=true | all-gather | bytes 17408 | tf_op jit(solution)/shard_map/all_gather | solution.py:98
  496.6 25.7 %all-gather.20.cloned.1.call-done = bf16[1,2048,256]{1,2,0:T(8,128)(2,1)} async-done(((bf16[1,128,256]{1,2,0:T(8,128)(2,1)}), bf16[1,2048,256]{1,2,0:T(8,128)(2,1)}) %all-gather.20.cloned.1.call-update) | async-done | bytes 1048592 | tf_op jit(solution)/shard_map/all_gather | solution.py:96
  522.3 0.0 copy-start.2
  522.3 3.6 fusion.8
  525.8 0.6 stack.2
  526.5 6.9 all-to-all-start
  533.4 0.0 copy-done.2
  533.4 3.0 fusion.21
  536.4 1.7 copy.59
  538.2 71.8 %all-gather.14.cloned.1.call-done = bf16[2048,256]{1,0:T(8,128)(2,1)} async-done(((bf16[128,256]{1,0:T(8,128)(2,1)}), bf16[2048,256]{1,0:T(8,128)(2,1)}) %all-gather.14.cloned.1.call-update) | async-done | bytes 1048592 | tf_op jit(solution)/shard_map/all_gather | solution.py:97
  609.9 1.5 copy.72
  611.4 0.0 all-to-all-done
  611.4 0.0 copy-done.1
  611.4 1.9 fusion.23
  613.4 0.7 copy.60
  614.1 0.4 convolution_convert_fusion.1
  614.6 0.7 copy.61
  615.3 2.9 fusion.24
  618.2 168.3 %reduce-scatter.5.cloned.1.call-done = f32[128,192]{0,1:T(8,128)} async-done(((f32[4096,192]{0,1:T(8,128)}), f32[128,192]{0,1:T(8,128)}) %reduce-scatter.5.cloned.1.call-update) | async-done | bytes 98320 | tf_op jit(solution)/shard_map/reduce_scatter | solution.py:123
  (6 shorter events, 0.1 us)
Async XLA Ops:
  7.2 82.1 %copy-start = (bf16[1,128,192]{1,2,0:T(8,128)(2,1)S(1)}, bf16[1,128,192]{1,2,0:T(8,128)(2,1)}, u32[]{:S(2)}) copy-start(bf16[1,128,192]{1,2,0:T(8,128)(2,1)} %param.9) | copy-start | bytes 147460
  7.2 85.0 %copy-start.4 = (bf16[1,128,256]{2,1,0:T(8,128)(2,1)S(1)}, bf16[1,128,256]{2,1,0:T(8,128)(2,1)}, u32[]{:S(2)}) copy-start(bf16[1,128,256]{2,1,0:T(8,128)(2,1)} %param.5) | copy-start | bytes 196612
  7.2 82.0 %all-gather.12.cloned.1.call-start = ((), (), s32[]{:S(2)}) async-start(), calls=%async_computation.4 | async-start | bytes 1671168 | tf_op jit(solution)/shard_map/all_gather | solution.py:62
  7.9 169.4 %all-gather.18.cloned.1.call-start = ((), (), s32[]{:S(2)}) async-start(), calls=%async_computation.9 | async-start | bytes 1114112 | tf_op jit(solution)/shard_map/all_gather | solution.py:39
  8.7 246.6 %all-gather.16.cloned.1.call-start = ((), (), s32[]{:S(2)}) async-start(), calls=%async_computation.8 | async-start | bytes 1114112 | tf_op jit(solution)/shard_map/all_gather | solution.py:38
  10.3 369.5 %reduce-scatter.3.cloned.1.call-start = ((), (), s32[]{:S(2)}) async-start(), calls=%async_computation.5 | async-start | bytes 1114112 | tf_op jit(solution)/shard_map/reduce_scatter | solution.py:71
  92.1 365.3 %all-gather.10.cloned.1.call-start = ((), (), s32[]{:S(2)}) async-start(), calls=%async_computation.3 | async-start | bytes 1114112 | tf_op jit(solution)/shard_map/all_gather | solution.py:58
  178.9 202.6 %copy-start.3 = (bf16[1,2048,256]{1,2,0:T(8,128)(2,1)}, bf16[1,2048,256]{1,2,0:T(8,128)(2,1)S(1)}, u32[]{:S(2)}) copy-start(bf16[1,2048,256]{1,2,0:T(8,128)(2,1)S(1)} %copy.43) | copy-start | bytes 3145732
  381.4 3.2 copy-start.5
  384.6 137.7 %all-gather.20.cloned.1.call-start = ((), (), s32[]{:S(2)}) async-start(), calls=%async_computation.10 | async-start | bytes 1114112 | tf_op jit(solution)/shard_map/all_gather | solution.py:96
  385.4 224.5 %all-gather.14.cloned.1.call-start = ((), (), s32[]{:S(2)}) async-start(), calls=%async_computation.6 | async-start | bytes 1114112 | tf_op jit(solution)/shard_map/all_gather | solution.py:97
  386.2 400.3 %reduce-scatter.5.cloned.1.call-start = ((), (), s32[]{:S(2)}) async-start(), calls=%async_computation.7 | async-start | bytes 3244032 | tf_op jit(solution)/shard_map/reduce_scatter | solution.py:123
  460.8 0.8 copy-start.6
  460.8 1.5 copy-start.7
  522.3 11.1 %copy-start.2 = (bf16[1,2048,256]{1,2,0:T(8,128)(2,1)S(1)}, bf16[1,2048,256]{1,2,0:T(8,128)(2,1)}, u32[]{:S(2)}) copy-start(bf16[1,2048,256]{1,2,0:T(8,128)(2,1)} %all-gather.16.cloned.1.call-done) | copy-start | bytes 3145732
  526.5 85.0 %all-to-all-start = ((f32[16,128,2]{1,2,0:T(2,128)}), f32[16,128,2]{1,2,0:T(2,128)S(1)}, u32[]{:S(2)}, u32[]{:S(2)}) async-start(f32[16,128,2]{1,2,0:T(2,128)} %stack.2), calls=%async_computation.1 | async-start | bytes 32768 | tf_op jit(solution)/shard_map/all_to_all | solution.py:100
  536.4 75.0 %copy-start.1 = (f32[2048,2,128]{0,2,1:T(8,128)S(1)}, f32[2048,2,128]{0,2,1:T(8,128)}, u32[]{:S(2)}) copy-start(f32[2048,2,128]{0,2,1:T(8,128)} %fusion.8) | copy-start | bytes 6291460
Sparse Core Ops, SparseCore 0:
  10.0 79.1 all-gather.11
  91.3 86.0 all-gather.17
  179.9 75.2 all-gather.15
  259.2 120.6 reduce-scatter.2
  384.7 72.6 all-gather.9
  460.0 62.2 all-gather.19
  524.6 85.3 all-gather.13
  613.6 172.8 reduce-scatter.4
